TPU v7x, 128 devices: a whole 4x4x4 slice. The times are simulated.
128 devices in a mesh: lat: 4 (over z_hi, core), lon: 32 (over y, z_lo, x).
Axes of the slice: x: 4, y: 4, z: 4 (z_hi: 2, z_lo: 2; z = z_hi * 2 + z_lo), core: 2. Of those that a mesh axis runs over, the one named last changes fastest.
Arguments:
- features: bfloat16 [8, 128, 1024, 256], P(None, 'lat', 'lon'), may hold values from -16 to 16
- band_points: int32 [128], replicated, may hold values from 256 to 1024, as said below
- survival_flags: int32 [8, 2], replicated, may hold values 0 or 1
- first_kernel_weight: bfloat16 [3, 3, 256, 256], replicated, may hold values from -0.125 to 0.125
- second_kernel_weight: bfloat16 [3, 3, 256, 256], replicated, may hold values from -0.125 to 0.125
Outputs:
- section_result: bfloat16 [8, 128, 1024, 256], P(None, 'lat', 'lon')
Inputs may be any that keep to these rules, and one draw needn't show every extreme that they name: `band_points`: the live points of a row are its first ones.
All inputs are finite; a program needn't handle non-finite values.
Results may differ from a plain program's by a relative error of at most 0.0006.
The roundings to bfloat16 on the way count: a program that leaves them out, or rounds other values in their place, can miss the bound.
Values may be sent and summed in bfloat16 or wider, within the bound.
No kernel may reach another device: no remote copies, remote signals or barrier semaphores. Data moves between devices by JAX's collectives and lax.ppermute only.
A program may use at most 320 MiB of HBM per device.

v0:
```python
import jax
import jax.numpy as jnp
from jax import lax
from jax.sharding import PartitionSpec as P

GROUPS = 32
FIRST_DILATION = 2
SECOND_DILATION = 4
EPS = 1e-05
KEEP_RATE = 0.8


def extended(array, sides, width, wrap):
    for axis, dim in sides:
        peers, length = (lax.axis_size(axis), array.shape[dim])
        up = [(i, (i + 1) % peers) for i in range(peers if wrap else peers - 1)]
        down = [(j, i) for i, j in up]
        last = lax.slice_in_dim(array, length - width, length, axis=dim)
        leading = lax.slice_in_dim(array, 0, width, axis=dim)
        before = lax.ppermute(last, axis, up)
        after = lax.ppermute(leading, axis, down)
        array = jnp.concatenate([before, array, after], axis=dim)
    return array


def widen_border(field_in, reach_cells):
    lat_padded = extended(field_in, (("lat", 1),), reach_cells, False)
    return extended(lat_padded, (("lon", 2),), reach_cells, True)


def live_cells(band_points, tile_rows, tile_cols, margin):
    lat_total = band_points.shape[0]
    lon_total = tile_cols * lax.axis_size("lon")
    row_index = (
        lax.axis_index("lat") * tile_rows
        - margin
        + jnp.arange(tile_rows + 2 * margin, dtype=jnp.int32)
    )
    col_index = (
        lax.axis_index("lon") * tile_cols
        - margin
        + jnp.arange(tile_cols + 2 * margin, dtype=jnp.int32)
    )
    col_index = jnp.mod(col_index, lon_total)
    matches = row_index[:, None] == jnp.arange(lat_total, dtype=jnp.int32)[None, :]
    row_points = jnp.sum(jnp.where(matches, band_points[None, :], 0), axis=1)
    return (col_index[None, :] < row_points[:, None]).astype(jnp.float32)


def statistics(values_in, live_mask, live_count, group_size):
    samples = values_in.shape[0]
    masked = values_in * live_mask[None, :, :, None]

    def group_total(chan_sums):
        return chan_sums.reshape(samples, GROUPS, group_size).sum(axis=2)

    group_means = lax.psum(group_total(jnp.sum(masked, axis=(1, 2))), ("lat", "lon")) / live_count
    shifted = values_in - jnp.repeat(group_means, group_size, axis=1)[:, None, None, :]
    squares = shifted * shifted * live_mask[None, :, :, None]
    group_vars = lax.psum(group_total(jnp.sum(squares, axis=(1, 2))), ("lat", "lon")) / live_count
    return (group_means, group_vars)


def activate(values_in, group_means, group_vars, live_mask, group_size):
    centre = jnp.repeat(group_means, group_size, axis=1)[:, None, None, :]
    inv_std = jnp.repeat(lax.rsqrt(group_vars + EPS), group_size, axis=1)[:, None, None, :]
    return (jax.nn.silu((values_in - centre) * inv_std) * live_mask[None, :, :, None]).astype(
        jnp.bfloat16
    )


def apply_kernel(padded, weight, dilation):
    out_rows = padded.shape[1] - 2 * dilation
    out_cols = padded.shape[2] - 2 * dilation
    summed = None
    for row_tap in range(3):
        for col_tap in range(3):
            shifted = padded[
                :,
                row_tap * dilation : row_tap * dilation + out_rows,
                col_tap * dilation : col_tap * dilation + out_cols,
                :,
            ]
            tap_term = jnp.einsum(
                "bijc,cd->bijd",
                shifted,
                weight[row_tap, col_tap],
                preferred_element_type=jnp.float32,
            )
            summed = tap_term if summed is None else summed + tap_term
    return summed


def residual_branch(padded, weight, dilation, kept):
    result = apply_kernel(padded, weight, dilation)
    return result * (kept.astype(jnp.float32) / KEEP_RATE)[:, None, None, None]


def per_device(features, band_points, survival_flags, first_kernel_weight, second_kernel_weight):
    tile_rows = features.shape[1]
    tile_cols = features.shape[2]
    group_size = features.shape[3] // GROUPS
    live_count = jnp.sum(band_points).astype(jnp.float32) * group_size
    live_inner = live_cells(band_points, tile_rows, tile_cols, 0)
    initial_feature_map = features.astype(jnp.float32)
    first_means, first_vars = statistics(initial_feature_map, live_inner, live_count, group_size)
    first_hidden = activate(initial_feature_map, first_means, first_vars, live_inner, group_size)
    first_result = (
        initial_feature_map
        + residual_branch(
            widen_border(first_hidden, FIRST_DILATION),
            first_kernel_weight,
            FIRST_DILATION,
            survival_flags[:, 0],
        )
    ).astype(jnp.bfloat16)
    first_result = lax.optimization_barrier(first_result)
    first_feature_map = first_result.astype(jnp.float32)
    second_means, second_vars = statistics(first_feature_map, live_inner, live_count, group_size)
    second_hidden = activate(first_feature_map, second_means, second_vars, live_inner, group_size)
    section_result = first_feature_map + residual_branch(
        widen_border(second_hidden, SECOND_DILATION),
        second_kernel_weight,
        SECOND_DILATION,
        survival_flags[:, 1],
    )
    return section_result.astype(jnp.bfloat16)


def solution(mesh):
    in_specs = (P(None, "lat", "lon", None), P(), P(), P(), P())
    out_specs = P(None, "lat", "lon", None)
    return jax.shard_map(
        per_device, mesh=mesh, in_specs=in_specs, out_specs=out_specs, check_vma=False
    )
```

profile of v0, /device:TPU:1, one launch (start us, length us, event | category | flops | bytes accessed | tf_op | source)
XLA Modules:
  0.0 468.8 jit_solution(17577725118338050617)
XLA Ops:
  4.2 68.7 %psum.28 = f32[8,32]{1,0:T(8,128)S(1)} all-reduce(f32[8,32]{1,0:T(8,128)S(1)} %reduce_sum.92), channel_id=1, replica_groups=mesh['lat'=4,'lon'=32] {'lat','lon'}, use_global_device_ids=true, to_apply=%region_3.4 | all-reduce | flops 256 | bytes 2048 | tf_op jit(solution)/shard_map/psum | solution.py:57
  79.0 62.6 %psum.29 = f32[8,32]{1,0:T(8,128)S(1)} all-reduce(f32[8,32]{1,0:T(8,128)S(1)} %reduce_sum.95), channel_id=1, replica_groups=mesh['lat'=4,'lon'=32] {'lat','lon'}, use_global_device_ids=true, to_apply=%region_7.8 | all-reduce | flops 256 | bytes 2048 | tf_op jit(solution)/shard_map/psum | solution.py:60
  152.0 4.5 fusion.84
  160.8 5.2 %collective-permute-start.3 = (bf16[8,36,2,256]{3,2,1,0:T(2,128)(2,1)S(1)}, bf16[8,36,2,256]{3,2,1,0:T(2,128)(2,1)S(1)}, u32[]{:S(2)}, u32[]{:S(2)}) collective-permute-start(bf16[8,36,2,256]{3,2,1,0:T(2,128)(2,1)S(1)} %get-tuple-element.11), channel_id=1, source_target_pairs={{1,0},{2,1},{3,2},{4,3},{5,4},{6,5},{7,6},{8,7},{9,8},{10,9},{11,1... | collective-permute-start | bytes 884744 | tf_op jit(solution)/shard_map/ppermute | solution.py:21
  170.4 4.5 fusion.38
  174.9 7.4 %pad_maximum_fusion.1 = (bf16[8,36,34,256]{3,2,1,0:T(8,128)(2,1)S(1)}, bf16[8,36,34,256]{3,2,1,0:T(8,128)(2,1)S(1)}) fusion(bf16[8,36,2,256]{3,2,1,0:T(2,128)(2,1)S(1)} %collective-permute-done.3, bf16[8,2,32,256]{3,2,1,0:T(8,128)(2,1)S(1)} %collective-permute-done.1, bf16[8,32,32,256]{3,2,1,0:T(8,128)(2,1)S(1)} %fusion.12, ...), kind=kLoop, calls=%fused_computation.35 | loop fusion | flops 40108032 | bytes 15335424 | tf_op jit(solution)/shard_map/concatenate | solution.py:22
  182.3 4.9 %fusion.56 = f32[8,32,32,256]{3,2,1,0:T(8,128)} fusion(bf16[8,36,34,256]{3,2,1,0:T(8,128)(2,1)S(1)} %get-tuple-element.10, bf16[3,3,256,256]{3,2,1,0:T(8,128)(2,1)S(1)} %copy-done.2), kind=kOutput, calls=%fused_computation.66 | convolution fusion | flops 1073741824 | bytes 12713984 | tf_op jit(solution)/shard_map/bijc,cd->bijd/dot_general | solution.py:84
  191.6 4.5 fusion.58
  196.1 4.5 fusion.62
  200.6 4.5 fusion.64
  205.1 26.7 %fusion.23 = bf16[8,32,32,256]{3,2,1,0:T(8,128)(2,1)} fusion(bf16[8,32,32,256]{3,2,1,0:T(8,128)(2,1)} %param.5, f32[8,32,32,256]{3,2,1,0:T(8,128)} %fusion.38, f32[8,32,32,256]{3,2,1,0:T(8,128)} %fusion.56, f32[8,32,32,256]{3,2,1,0:T(8,128)} %fusion.58, f32[8,32,32,256]{3,2,1,0:T(8,128)} %fusion.84, f32[8,32,32,256]{3,2,1,0:T(8,128)} %fusion.60, ...), kind=kOutput, calls=%fused_computation.29 | convolution fusion | flops 1098907648 | bytes 79823360 | tf_op jit(solution)/shard_map/bijc,cd->bijd/dot_general | solution.py:84
  235.1 62.3 %psum.30 = f32[8,32]{1,0:T(8,128)S(1)} all-reduce(f32[8,32]{1,0:T(8,128)S(1)} %reduce_sum.97), channel_id=1, replica_groups=mesh['lat'=4,'lon'=32] {'lat','lon'}, use_global_device_ids=true, to_apply=%region_10.11 | all-reduce | flops 256 | bytes 2048 | tf_op jit(solution)/shard_map/psum | solution.py:57
  301.5 62.9 %psum.31 = f32[8,32]{1,0:T(8,128)S(1)} all-reduce(f32[8,32]{1,0:T(8,128)S(1)} %reduce_sum.99), channel_id=1, replica_groups=mesh['lat'=4,'lon'=32] {'lat','lon'}, use_global_device_ids=true, to_apply=%region_13.14 | all-reduce | flops 256 | bytes 2048 | tf_op jit(solution)/shard_map/psum | solution.py:60
  375.0 4.5 fusion.74
  379.5 19.6 %collective-permute-done.5 = bf16[8,4,32,256]{3,2,1,0:T(8,128)(2,1)S(1)} collective-permute-done((bf16[8,4,32,256]{3,2,1,0:T(8,128)(2,1)S(1)}, bf16[8,4,32,256]{3,2,1,0:T(8,128)(2,1)S(1)}, u32[]{:S(2)}, u32[]{:S(2)}) %collective-permute-start.5) | collective-permute-done | bytes 524320 | tf_op jit(solution)/shard_map/ppermute | solution.py:21
  399.8 5.9 %collective-permute-start.7 = (bf16[8,40,4,256]{3,2,1,0:T(4,128)(2,1)S(1)}, bf16[8,40,4,256]{3,2,1,0:T(4,128)(2,1)S(1)}, u32[]{:S(2)}, u32[]{:S(2)}) collective-permute-start(bf16[8,40,4,256]{3,2,1,0:T(4,128)(2,1)S(1)} %get-tuple-element.7), channel_id=1, source_target_pairs={{1,0},{2,1},{3,2},{4,3},{5,4},{6,5},{7,6},{8,7},{9,8},{10,9},{11,1... | collective-permute-start | bytes 1966088 | tf_op jit(solution)/shard_map/ppermute | solution.py:21
  410.1 4.5 fusion.30
  414.6 4.5 pad_maximum_fusion
  419.1 4.9 %fusion.44 = f32[8,32,32,256]{3,2,1,0:T(8,128)} fusion(bf16[8,40,36,256]{3,2,1,0:T(8,128)(2,1)S(1)} %get-tuple-element.6, bf16[3,3,256,256]{3,2,1,0:T(8,128)(2,1)S(1)} %copy-done.3), kind=kOutput, calls=%fused_computation.54 | convolution fusion | flops 1073741824 | bytes 12713984 | tf_op jit(solution)/shard_map/bijc,cd->bijd/dot_general | solution.py:84
  424.0 4.5 fusion.48
  428.4 4.5 fusion.46
  432.9 4.5 fusion.50
  437.4 4.5 fusion.52
  441.9 26.7 %fusion.25 = bf16[8,32,32,256]{3,2,1,0:T(8,128)(2,1)} fusion(bf16[8,32,32,256]{3,2,1,0:T(8,128)(2,1)} %fusion.23, f32[8,32,32,256]{3,2,1,0:T(8,128)} %fusion.30, f32[8,32,32,256]{3,2,1,0:T(8,128)} %fusion.44, f32[8,32,32,256]{3,2,1,0:T(8,128)} %fusion.46, f32[8,32,32,256]{3,2,1,0:T(8,128)} %fusion.74, f32[8,32,32,256]{3,2,1,0:T(8,128)} %fusion.48, ...), kind=kOutput, calls=%fused_computation.31 | convolution fusion | flops 1098907648 | bytes 79823360 | tf_op jit(solution)/shard_map/bijc,cd->bijd/dot_general | solution.py:84
  (62 shorter events, 56.1 us)
Async XLA Ops:
  75.1 76.9 %copy-start.2 = (bf16[3,3,256,256]{3,2,1,0:T(8,128)(2,1)S(1)}, bf16[3,3,256,256]{3,2,1,0:T(8,128)(2,1)}, u32[]{:S(2)}) copy-start(bf16[3,3,256,256]{3,2,1,0:T(8,128)(2,1)} %param.8) | copy-start | bytes 3538948
  146.2 10.3 %collective-permute-start = (bf16[8,2,32,256]{3,2,1,0:T(8,128)(2,1)S(1)}, bf16[8,2,32,256]{3,2,1,0:T(8,128)(2,1)S(1)}, u32[]{:S(2)}, u32[]{:S(2)}) collective-permute-start(bf16[8,2,32,256]{3,2,1,0:T(8,128)(2,1)S(1)} %get-tuple-element.15), channel_id=1, source_target_pairs={{0,32},{32,64},{64,96},{1,33},{33,65},{65,97},{2,34},{34,66},{66,9... | collective-permute-start | bytes 786440 | tf_op jit(solution)/shard_map/ppermute | solution.py:20
  150.1 6.4 %copy-start.4 = (s32[8,2]{0,1:T(2,128)S(1)}, s32[8,2]{0,1:T(2,128)}, u32[]{:S(2)}) copy-start(s32[8,2]{0,1:T(2,128)} %param.7) | copy-start | bytes 196
  150.1 9.2 %collective-permute-start.1 = (bf16[8,2,32,256]{3,2,1,0:T(8,128)(2,1)S(1)}, bf16[8,2,32,256]{3,2,1,0:T(8,128)(2,1)S(1)}, u32[]{:S(2)}, u32[]{:S(2)}) collective-permute-start(bf16[8,2,32,256]{3,2,1,0:T(8,128)(2,1)S(1)} %get-tuple-element.16), channel_id=1, source_target_pairs={{32,0},{64,32},{96,64},{33,1},{65,33},{97,65},{34,2},{66,34},{98,6... | collective-permute-start | bytes 786440 | tf_op jit(solution)/shard_map/ppermute | solution.py:21
  159.7 15.1 %collective-permute-start.2 = (bf16[8,36,2,256]{3,2,1,0:T(2,128)(2,1)S(1)}, bf16[8,36,2,256]{3,2,1,0:T(2,128)(2,1)S(1)}, u32[]{:S(2)}, u32[]{:S(2)}) collective-permute-start(bf16[8,36,2,256]{3,2,1,0:T(2,128)(2,1)S(1)} %get-tuple-element.12), channel_id=1, source_target_pairs={{0,1},{1,2},{2,3},{3,4},{4,5},{5,6},{6,7},{7,8},{8,9},{9,10},{10,1... | collective-permute-start | bytes 884744 | tf_op jit(solution)/shard_map/ppermute | solution.py:20
  160.8 14.1 %collective-permute-start.3 = (bf16[8,36,2,256]{3,2,1,0:T(2,128)(2,1)S(1)}, bf16[8,36,2,256]{3,2,1,0:T(2,128)(2,1)S(1)}, u32[]{:S(2)}, u32[]{:S(2)}) collective-permute-start(bf16[8,36,2,256]{3,2,1,0:T(2,128)(2,1)S(1)} %get-tuple-element.11), channel_id=1, source_target_pairs={{1,0},{2,1},{3,2},{4,3},{5,4},{6,5},{7,6},{8,7},{9,8},{10,9},{11,1... | collective-permute-start | bytes 884744 | tf_op jit(solution)/shard_map/ppermute | solution.py:21
  182.3 13.8 %copy-start = (bf16[8,36,34,256]{3,2,1,0:T(8,128)(2,1)}, bf16[8,36,34,256]{3,2,1,0:T(8,128)(2,1)S(1)}, u32[]{:S(2)}) copy-start(bf16[8,36,34,256]{3,2,1,0:T(8,128)(2,1)S(1)} %get-tuple-element.9) | copy-start | bytes 15040516
  301.2 73.8 %copy-start.3 = (bf16[3,3,256,256]{3,2,1,0:T(8,128)(2,1)S(1)}, bf16[3,3,256,256]{3,2,1,0:T(8,128)(2,1)}, u32[]{:S(2)}) copy-start(bf16[3,3,256,256]{3,2,1,0:T(8,128)(2,1)} %param.9) | copy-start | bytes 3538948
  369.0 10.5 %collective-permute-start.4 = (bf16[8,4,32,256]{3,2,1,0:T(8,128)(2,1)S(1)}, bf16[8,4,32,256]{3,2,1,0:T(8,128)(2,1)S(1)}, u32[]{:S(2)}, u32[]{:S(2)}) collective-permute-start(bf16[8,4,32,256]{3,2,1,0:T(8,128)(2,1)S(1)} %get-tuple-element.13), channel_id=1, source_target_pairs={{0,32},{32,64},{64,96},{1,33},{33,65},{65,97},{2,34},{34,66},{66,9... | collective-permute-start | bytes 1572872 | tf_op jit(solution)/shard_map/ppermute | solution.py:20
  373.1 26.0 %collective-permute-start.5 = (bf16[8,4,32,256]{3,2,1,0:T(8,128)(2,1)S(1)}, bf16[8,4,32,256]{3,2,1,0:T(8,128)(2,1)S(1)}, u32[]{:S(2)}, u32[]{:S(2)}) collective-permute-start(bf16[8,4,32,256]{3,2,1,0:T(8,128)(2,1)S(1)} %get-tuple-element.14), channel_id=1, source_target_pairs={{32,0},{64,32},{96,64},{33,1},{65,33},{97,65},{34,2},{66,34},{98,6... | collective-permute-start | bytes 1572872 | tf_op jit(solution)/shard_map/ppermute | solution.py:21
  399.7 14.9 %collective-permute-start.6 = (bf16[8,40,4,256]{3,2,1,0:T(4,128)(2,1)S(1)}, bf16[8,40,4,256]{3,2,1,0:T(4,128)(2,1)S(1)}, u32[]{:S(2)}, u32[]{:S(2)}) collective-permute-start(bf16[8,40,4,256]{3,2,1,0:T(4,128)(2,1)S(1)} %get-tuple-element.8), channel_id=1, source_target_pairs={{0,1},{1,2},{2,3},{3,4},{4,5},{5,6},{6,7},{7,8},{8,9},{9,10},{10,1... | collective-permute-start | bytes 1966088 | tf_op jit(solution)/shard_map/ppermute | solution.py:20
  399.8 14.8 %collective-permute-start.7 = (bf16[8,40,4,256]{3,2,1,0:T(4,128)(2,1)S(1)}, bf16[8,40,4,256]{3,2,1,0:T(4,128)(2,1)S(1)}, u32[]{:S(2)}, u32[]{:S(2)}) collective-permute-start(bf16[8,40,4,256]{3,2,1,0:T(4,128)(2,1)S(1)} %get-tuple-element.7), channel_id=1, source_target_pairs={{1,0},{2,1},{3,2},{4,3},{5,4},{6,5},{7,6},{8,7},{9,8},{10,9},{11,1... | collective-permute-start | bytes 1966088 | tf_op jit(solution)/shard_map/ppermute | solution.py:21
  419.1 13.8 %copy-start.1 = (bf16[8,40,36,256]{3,2,1,0:T(8,128)(2,1)}, bf16[8,40,36,256]{3,2,1,0:T(8,128)(2,1)S(1)}, u32[]{:S(2)}) copy-start(bf16[8,40,36,256]{3,2,1,0:T(8,128)(2,1)S(1)} %get-tuple-element.5) | copy-start | bytes 17694724
where the time goes:
time: 476 us; the launch traced here: 469 us
  blocking collectives  257 us (54%)
  matrix products  126 us (26%)
  other arithmetic  37.6 us (8%)
  starting transfers between devices  23.9 us (5%)
  waiting for transfers between devices  22.4 us (5%)
    psum x2, blocking collectives, statistics(): lax.psum(group_total(jnp.sum(masked, axis=(1, 2))), ('lat', 'lon'))  131 us
    dot_general x18, matrix products, apply_kernel(): jnp.einsum('bijc,cd->bijd', shifted, weight[row_tap, col_tap], preferred_...  126 us
    psum x2, blocking collectives, statistics(): lax.psum(group_total(jnp.sum(squares, axis=(1, 2))), ('lat', 'lon'))  125 us
    ppermute x4, waiting for transfers between devices, extended(): after = lax.ppermute(leading, axis, down)  22.4 us
    ppermute x4, starting transfers between devices, extended(): after = lax.ppermute(leading, axis, down)  14.9 us
    concatenate x4, other arithmetic, extended(): array = jnp.concatenate([before, array, after], axis=dim)  13 us
  transfers between devices with their start and end apart: 8, of which 2 were waited for; matrix products, arithmetic and copies ran while one was open for 6% of the time, Pallas kernels for 0%

commit v1 on v0

--- a/solution.py
+++ b/solution.py
@@ -54,7 +54,9 @@
     def group_total(chan_sums):
         return chan_sums.reshape(samples, GROUPS, group_size).sum(axis=2)
 
-    group_means = lax.psum(group_total(jnp.sum(masked, axis=(1, 2))), ("lat", "lon")) / live_count
+    group_means = (
+        lax.psum(lax.psum(group_total(jnp.sum(masked, axis=(1, 2))), "lat"), "lon") / live_count
+    )
     shifted = values_in - jnp.repeat(group_means, group_size, axis=1)[:, None, None, :]
     squares = shifted * shifted * live_mask[None, :, :, None]
     group_vars = lax.psum(group_total(jnp.sum(squares, axis=(1, 2))), ("lat", "lon")) / live_count

time: 476 us -> 525 us (1.10)
  blocking collectives: 257 us -> 304 us
    psum x2, blocking collectives: 125 us -> 157 us  [statistics(): lax.psum(group_total(jnp.sum(squares, axis=(1, 2))), ('lat', 'lon'))]
    psum x2 -> x4, blocking collectives: 131 us -> 148 us  [the longest x2 132 us: statistics(): lax.psum(lax.psum(group_total(jnp.sum(masked, axis=(1, 2))), 'lat'), 'lon')]
  transfers between devices with their start and end apart: 8 -> 8, of which waited for: 2 -> 2; matrix products, arithmetic and copies ran while one was open for 6% -> 5% of each run, Pallas kernels for 0% -> 0%
where the time goes in v1:
time: 525 us; the launch traced here: 518 us
  blocking collectives  304 us (58%)
  matrix products  126 us (24%)
  other arithmetic  37.6 us (7%)
  starting transfers between devices  25 us (5%)
  waiting for transfers between devices  22.4 us (4%)
    psum x2, blocking collectives, statistics(): lax.psum(group_total(jnp.sum(squares, axis=(1, 2))), ('lat', 'lon'))  157 us
    psum x2, blocking collectives, statistics(): lax.psum(lax.psum(group_total(jnp.sum(masked, axis=(1, 2))), 'lat'), 'lon')  132 us
    dot_general x18, matrix products, apply_kernel(): jnp.einsum('bijc,cd->bijd', shifted, weight[row_tap, col_tap], preferred_...  126 us
    ppermute x4, waiting for transfers between devices, extended(): after = lax.ppermute(leading, axis, down)  22.4 us
    ppermute x4, starting transfers between devices, extended(): after = lax.ppermute(leading, axis, down)  15.8 us
    psum x2, blocking collectives, statistics(): lax.psum(group_total(jnp.sum(masked, axis=(1, 2))), 'lat')  15.6 us
    concatenate x4, other arithmetic, extended(): array = jnp.concatenate([before, array, after], axis=dim)  13 us
  transfers between devices with their start and end apart: 8, of which 2 were waited for; matrix products, arithmetic and copies ran while one was open for 5% of the time, Pallas kernels for 0%

profile of v1, /device:TPU:1, one launch (start us, length us, event | category | flops | bytes accessed | tf_op | source)
XLA Modules:
  0.0 517.9 jit_solution(14304971302876323023)
XLA Ops:
  4.2 8.8 %psum.42 = f32[8,32]{1,0:T(8,128)S(1)} all-reduce(f32[8,32]{1,0:T(8,128)S(1)} %reduce_sum.92), channel_id=1, replica_groups=mesh['lat'=4,'lon'=32] {'lat'}, use_global_device_ids=true, to_apply=%region_3.4 | all-reduce | flops 256 | bytes 2048 | tf_op jit(solution)/shard_map/psum | solution.py:58
  13.0 68.4 %psum.43 = f32[8,32]{1,0:T(8,128)S(1)} all-reduce(f32[8,32]{1,0:T(8,128)S(1)} %psum.42), channel_id=1, replica_groups=mesh['lat'=4,'lon'=32] {'lon'}, use_global_device_ids=true, to_apply=%region_4.5 | all-reduce | flops 256 | bytes 2048 | tf_op jit(solution)/shard_map/psum | solution.py:58
  87.5 79.0 %psum.44 = f32[8,32]{1,0:T(8,128)S(1)} all-reduce(f32[8,32]{1,0:T(8,128)S(1)} %reduce_sum.95), channel_id=1, replica_groups=mesh['lat'=4,'lon'=32] {'lat','lon'}, use_global_device_ids=true, to_apply=%region_8.9 | all-reduce | flops 256 | bytes 2048 | tf_op jit(solution)/shard_map/psum | solution.py:62
  177.2 4.5 fusion.84
  185.0 6.1 %collective-permute-start.3 = (bf16[8,36,2,256]{3,2,1,0:T(2,128)(2,1)S(1)}, bf16[8,36,2,256]{3,2,1,0:T(2,128)(2,1)S(1)}, u32[]{:S(2)}, u32[]{:S(2)}) collective-permute-start(bf16[8,36,2,256]{3,2,1,0:T(2,128)(2,1)S(1)} %get-tuple-element.11), channel_id=1, source_target_pairs={{1,0},{2,1},{3,2},{4,3},{5,4},{6,5},{7,6},{8,7},{9,8},{10,9},{11,1... | collective-permute-start | bytes 884744 | tf_op jit(solution)/shard_map/ppermute | solution.py:21
  195.5 4.5 fusion.38
  200.0 7.4 %pad_maximum_fusion.1 = (bf16[8,36,34,256]{3,2,1,0:T(8,128)(2,1)S(1)}, bf16[8,36,34,256]{3,2,1,0:T(8,128)(2,1)S(1)}) fusion(bf16[8,36,2,256]{3,2,1,0:T(2,128)(2,1)S(1)} %collective-permute-done.3, bf16[8,2,32,256]{3,2,1,0:T(8,128)(2,1)S(1)} %collective-permute-done.1, bf16[8,32,32,256]{3,2,1,0:T(8,128)(2,1)S(1)} %fusion.12, ...), kind=kLoop, calls=%fused_computation.35 | loop fusion | flops 40108032 | bytes 15335424 | tf_op jit(solution)/shard_map/concatenate | solution.py:22
  207.5 4.9 fusion.56
  216.8 4.5 fusion.58
  221.3 4.5 fusion.62
  225.8 4.5 fusion.64
  230.2 26.7 %fusion.23 = bf16[8,32,32,256]{3,2,1,0:T(8,128)(2,1)} fusion(bf16[8,32,32,256]{3,2,1,0:T(8,128)(2,1)} %param.5, f32[8,32,32,256]{3,2,1,0:T(8,128)} %fusion.38, f32[8,32,32,256]{3,2,1,0:T(8,128)} %fusion.56, f32[8,32,32,256]{3,2,1,0:T(8,128)} %fusion.58, f32[8,32,32,256]{3,2,1,0:T(8,128)} %fusion.84, f32[8,32,32,256]{3,2,1,0:T(8,128)} %fusion.60, ...), kind=kOutput, calls=%fused_computation.29 | convolution fusion | flops 1098907648 | bytes 79823360 | tf_op jit(solution)/shard_map/bijc,cd->bijd/dot_general | solution.py:86
  260.3 6.8 %psum.45 = f32[8,32]{1,0:T(8,128)S(1)} all-reduce(f32[8,32]{1,0:T(8,128)S(1)} %reduce_sum.97), channel_id=1, replica_groups=mesh['lat'=4,'lon'=32] {'lat'}, use_global_device_ids=true, to_apply=%region_11.12 | all-reduce | flops 256 | bytes 2048 | tf_op jit(solution)/shard_map/psum | solution.py:58
  267.1 64.0 %psum.46 = f32[8,32]{1,0:T(8,128)S(1)} all-reduce(f32[8,32]{1,0:T(8,128)S(1)} %psum.45), channel_id=1, replica_groups=mesh['lat'=4,'lon'=32] {'lon'}, use_global_device_ids=true, to_apply=%region_12.13 | all-reduce | flops 256 | bytes 2048 | tf_op jit(solution)/shard_map/psum | solution.py:58
  335.1 77.5 %psum.47 = f32[8,32]{1,0:T(8,128)S(1)} all-reduce(f32[8,32]{1,0:T(8,128)S(1)} %reduce_sum.99), channel_id=1, replica_groups=mesh['lat'=4,'lon'=32] {'lat','lon'}, use_global_device_ids=true, to_apply=%region_15.16 | all-reduce | flops 256 | bytes 2048 | tf_op jit(solution)/shard_map/psum | solution.py:62
  417.2 5.0 collective-permute-start.4
  428.6 19.6 %collective-permute-done.5 = bf16[8,4,32,256]{3,2,1,0:T(8,128)(2,1)S(1)} collective-permute-done((bf16[8,4,32,256]{3,2,1,0:T(8,128)(2,1)S(1)}, bf16[8,4,32,256]{3,2,1,0:T(8,128)(2,1)S(1)}, u32[]{:S(2)}, u32[]{:S(2)}) %collective-permute-start.5) | collective-permute-done | bytes 524320 | tf_op jit(solution)/shard_map/ppermute | solution.py:21
  448.9 5.9 %collective-permute-start.7 = (bf16[8,40,4,256]{3,2,1,0:T(4,128)(2,1)S(1)}, bf16[8,40,4,256]{3,2,1,0:T(4,128)(2,1)S(1)}, u32[]{:S(2)}, u32[]{:S(2)}) collective-permute-start(bf16[8,40,4,256]{3,2,1,0:T(4,128)(2,1)S(1)} %get-tuple-element.7), channel_id=1, source_target_pairs={{1,0},{2,1},{3,2},{4,3},{5,4},{6,5},{7,6},{8,7},{9,8},{10,9},{11,1... | collective-permute-start | bytes 1966088 | tf_op jit(solution)/shard_map/ppermute | solution.py:21
  459.2 4.5 fusion.30
  463.7 4.5 pad_maximum_fusion
  468.2 4.9 fusion.44
  477.5 4.5 fusion.46
  482.1 4.5 fusion.50
  491.0 26.7 %fusion.25 = bf16[8,32,32,256]{3,2,1,0:T(8,128)(2,1)} fusion(bf16[8,32,32,256]{3,2,1,0:T(8,128)(2,1)} %fusion.23, f32[8,32,32,256]{3,2,1,0:T(8,128)} %fusion.30, f32[8,32,32,256]{3,2,1,0:T(8,128)} %fusion.44, f32[8,32,32,256]{3,2,1,0:T(8,128)} %fusion.46, f32[8,32,32,256]{3,2,1,0:T(8,128)} %fusion.74, f32[8,32,32,256]{3,2,1,0:T(8,128)} %fusion.48, ...), kind=kOutput, calls=%fused_computation.31 | convolution fusion | flops 1098907648 | bytes 79823360 | tf_op jit(solution)/shard_map/bijc,cd->bijd/dot_general | solution.py:86
  (64 shorter events, 64.7 us)
Async XLA Ops:
  83.6 93.6 %copy-start.2 = (bf16[3,3,256,256]{3,2,1,0:T(8,128)(2,1)S(1)}, bf16[3,3,256,256]{3,2,1,0:T(8,128)(2,1)}, u32[]{:S(2)}) copy-start(bf16[3,3,256,256]{3,2,1,0:T(8,128)(2,1)} %param.8) | copy-start | bytes 3538948
  171.1 10.5 %collective-permute-start = (bf16[8,2,32,256]{3,2,1,0:T(8,128)(2,1)S(1)}, bf16[8,2,32,256]{3,2,1,0:T(8,128)(2,1)S(1)}, u32[]{:S(2)}, u32[]{:S(2)}) collective-permute-start(bf16[8,2,32,256]{3,2,1,0:T(8,128)(2,1)S(1)} %get-tuple-element.15), channel_id=1, source_target_pairs={{0,32},{32,64},{64,96},{1,33},{33,65},{65,97},{2,34},{34,66},{66,9... | collective-permute-start | bytes 786440 | tf_op jit(solution)/shard_map/ppermute | solution.py:20
  175.2 6.4 %copy-start.4 = (s32[8,2]{0,1:T(2,128)S(1)}, s32[8,2]{0,1:T(2,128)}, u32[]{:S(2)}) copy-start(s32[8,2]{0,1:T(2,128)} %param.7) | copy-start | bytes 196
  175.2 9.2 %collective-permute-start.1 = (bf16[8,2,32,256]{3,2,1,0:T(8,128)(2,1)S(1)}, bf16[8,2,32,256]{3,2,1,0:T(8,128)(2,1)S(1)}, u32[]{:S(2)}, u32[]{:S(2)}) collective-permute-start(bf16[8,2,32,256]{3,2,1,0:T(8,128)(2,1)S(1)} %get-tuple-element.16), channel_id=1, source_target_pairs={{32,0},{64,32},{96,64},{33,1},{65,33},{97,65},{34,2},{66,34},{98,6... | collective-permute-start | bytes 786440 | tf_op jit(solution)/shard_map/ppermute | solution.py:21
  184.9 15.1 %collective-permute-start.2 = (bf16[8,36,2,256]{3,2,1,0:T(2,128)(2,1)S(1)}, bf16[8,36,2,256]{3,2,1,0:T(2,128)(2,1)S(1)}, u32[]{:S(2)}, u32[]{:S(2)}) collective-permute-start(bf16[8,36,2,256]{3,2,1,0:T(2,128)(2,1)S(1)} %get-tuple-element.12), channel_id=1, source_target_pairs={{0,1},{1,2},{2,3},{3,4},{4,5},{5,6},{6,7},{7,8},{8,9},{9,10},{10,1... | collective-permute-start | bytes 884744 | tf_op jit(solution)/shard_map/ppermute | solution.py:20
  185.0 15.0 %collective-permute-start.3 = (bf16[8,36,2,256]{3,2,1,0:T(2,128)(2,1)S(1)}, bf16[8,36,2,256]{3,2,1,0:T(2,128)(2,1)S(1)}, u32[]{:S(2)}, u32[]{:S(2)}) collective-permute-start(bf16[8,36,2,256]{3,2,1,0:T(2,128)(2,1)S(1)} %get-tuple-element.11), channel_id=1, source_target_pairs={{1,0},{2,1},{3,2},{4,3},{5,4},{6,5},{7,6},{8,7},{9,8},{10,9},{11,1... | collective-permute-start | bytes 884744 | tf_op jit(solution)/shard_map/ppermute | solution.py:21
  207.5 13.8 %copy-start = (bf16[8,36,34,256]{3,2,1,0:T(8,128)(2,1)}, bf16[8,36,34,256]{3,2,1,0:T(8,128)(2,1)S(1)}, u32[]{:S(2)}) copy-start(bf16[8,36,34,256]{3,2,1,0:T(8,128)(2,1)S(1)} %get-tuple-element.9) | copy-start | bytes 15040516
  334.9 89.2 %copy-start.3 = (bf16[3,3,256,256]{3,2,1,0:T(8,128)(2,1)S(1)}, bf16[3,3,256,256]{3,2,1,0:T(8,128)(2,1)}, u32[]{:S(2)}) copy-start(bf16[3,3,256,256]{3,2,1,0:T(8,128)(2,1)} %param.9) | copy-start | bytes 3538948
  417.2 11.4 %collective-permute-start.4 = (bf16[8,4,32,256]{3,2,1,0:T(8,128)(2,1)S(1)}, bf16[8,4,32,256]{3,2,1,0:T(8,128)(2,1)S(1)}, u32[]{:S(2)}, u32[]{:S(2)}) collective-permute-start(bf16[8,4,32,256]{3,2,1,0:T(8,128)(2,1)S(1)} %get-tuple-element.13), channel_id=1, source_target_pairs={{0,32},{32,64},{64,96},{1,33},{33,65},{65,97},{2,34},{34,66},{66,9... | collective-permute-start | bytes 1572872 | tf_op jit(solution)/shard_map/ppermute | solution.py:20
  422.2 26.0 %collective-permute-start.5 = (bf16[8,4,32,256]{3,2,1,0:T(8,128)(2,1)S(1)}, bf16[8,4,32,256]{3,2,1,0:T(8,128)(2,1)S(1)}, u32[]{:S(2)}, u32[]{:S(2)}) collective-permute-start(bf16[8,4,32,256]{3,2,1,0:T(8,128)(2,1)S(1)} %get-tuple-element.14), channel_id=1, source_target_pairs={{32,0},{64,32},{96,64},{33,1},{65,33},{97,65},{34,2},{66,34},{98,6... | collective-permute-start | bytes 1572872 | tf_op jit(solution)/shard_map/ppermute | solution.py:21
  448.8 14.9 %collective-permute-start.6 = (bf16[8,40,4,256]{3,2,1,0:T(4,128)(2,1)S(1)}, bf16[8,40,4,256]{3,2,1,0:T(4,128)(2,1)S(1)}, u32[]{:S(2)}, u32[]{:S(2)}) collective-permute-start(bf16[8,40,4,256]{3,2,1,0:T(4,128)(2,1)S(1)} %get-tuple-element.8), channel_id=1, source_target_pairs={{0,1},{1,2},{2,3},{3,4},{4,5},{5,6},{6,7},{7,8},{8,9},{9,10},{10,1... | collective-permute-start | bytes 1966088 | tf_op jit(solution)/shard_map/ppermute | solution.py:20
  448.9 14.8 %collective-permute-start.7 = (bf16[8,40,4,256]{3,2,1,0:T(4,128)(2,1)S(1)}, bf16[8,40,4,256]{3,2,1,0:T(4,128)(2,1)S(1)}, u32[]{:S(2)}, u32[]{:S(2)}) collective-permute-start(bf16[8,40,4,256]{3,2,1,0:T(4,128)(2,1)S(1)} %get-tuple-element.7), channel_id=1, source_target_pairs={{1,0},{2,1},{3,2},{4,3},{5,4},{6,5},{7,6},{8,7},{9,8},{10,9},{11,1... | collective-permute-start | bytes 1966088 | tf_op jit(solution)/shard_map/ppermute | solution.py:21
  468.2 13.8 %copy-start.1 = (bf16[8,40,36,256]{3,2,1,0:T(8,128)(2,1)}, bf16[8,40,36,256]{3,2,1,0:T(8,128)(2,1)S(1)}, u32[]{:S(2)}) copy-start(bf16[8,40,36,256]{3,2,1,0:T(8,128)(2,1)S(1)} %get-tuple-element.5) | copy-start | bytes 17694724
